TPU v7x, 256 devices: a whole 4x4x8 slice. The times are simulated.
256 devices in a mesh: context: 64 (over y, x_lo, z), heads: 4 (over x_hi, core).
Axes of the slice: x: 4 (x_hi: 2, x_lo: 2; x = x_hi * 2 + x_lo), y: 4, z: 8, core: 2. Of those that a mesh axis runs over, the one named last changes fastest.
Arguments:
- upstream: bfloat16 [16384, 1024], P(('context', 'heads')), may hold values from -48 to 48
- out_weight: bfloat16 [1024, 1024], P('heads'), may hold values from -0.1875 to 0.1875
- query_rows: bfloat16 [16384, 1024], P('context', 'heads'), may hold values from -6 to 6
- key_rows: bfloat16 [16384, 1024], P('context', 'heads'), may hold values from -6 to 6
- value_rows: bfloat16 [16384, 1024], P('context', 'heads'), may hold values from -6 to 6
- head_offsets: int32 [16], replicated, may hold values from 0 to 15, each once
Outputs:
- query_grad: bfloat16 [16384, 1024], P('context', 'heads')
- key_grad: bfloat16 [16384, 1024], P('context', 'heads')
- value_grad: bfloat16 [16384, 1024], P('context', 'heads')
Inputs may be any that keep to these rules, and one draw needn't show every extreme that they name: `head_offsets`: every value of 0 to 15 occurs once.
All inputs are finite; a program needn't handle non-finite values.
Results may differ from a plain program's by a relative error of at most 0.008.
Values may be sent and summed in bfloat16 or wider, within the bound.
A program may use at most 128 MiB of HBM per device.

v0:
```python
import math
import jax
import jax.numpy as jnp
from jax import lax
from jax.sharding import PartitionSpec as P

HEAD_SIZE = 64
DILATION_RATE = 16
FIRST_SEGMENT = 2048


def partner_2(value, axis, apart):
    mask = 2**apart
    pairs = [(source, source ^ mask) for source in range(lax.axis_size(axis))]
    return lax.ppermute(value, axis, pairs)


def dot_rows(left, right):
    return lax.dot_general(
        left, right, (((1,), (1,)), ((), ())), preferred_element_type=jnp.float32
    )


def dot_cols(left, right):
    return lax.dot_general(
        left, right, (((0,), (0,)), ((), ())), preferred_element_type=jnp.float32
    )


def pick_rows(payload_arrays, mask_stack):
    span_length, block_width = payload_arrays.shape
    head_count = mask_stack.shape[1]
    launch_layout = payload_arrays.reshape(
        span_length // DILATION_RATE, DILATION_RATE, head_count, block_width // head_count
    )
    selected_rows = jnp.where(
        mask_stack[None, :, :, None], launch_layout, jnp.zeros((), payload_arrays.dtype)
    )
    return jnp.sum(selected_rows, axis=1).reshape(span_length // DILATION_RATE, block_width)


def place_rows(picked, mask_stack):
    total_count, block_width = picked.shape
    head_count = mask_stack.shape[1]
    launch_layout = picked.reshape(total_count, 1, head_count, block_width // head_count)
    dispersal_rows = jnp.where(
        mask_stack[None, :, :, None], launch_layout, jnp.zeros((), picked.dtype)
    )
    return dispersal_rows.reshape(total_count * DILATION_RATE, block_width)


def spread_rows(value_tensor, head_shift):
    total_count = value_tensor.shape[0]
    matched_flag = jnp.arange(DILATION_RATE, dtype=jnp.int32)[None, :] == head_shift
    return jnp.where(
        matched_flag, value_tensor[:, None], jnp.zeros((), value_tensor.dtype)
    ).reshape(total_count * DILATION_RATE)


def double_up(buffer, levels, position):
    for level in range(levels):
        partner = partner_2(buffer, "context", level)
        lower = position >> level & 1 == 0
        buffer = jnp.where(
            lower, jnp.concatenate([buffer, partner], 1), jnp.concatenate([partner, buffer], 1)
        )
    return buffer


def halve_down(buffer, levels, position):
    for level in range(levels - 1, -1, -1):
        middle = buffer.shape[1] // 2
        lower_half = buffer[:, :middle]
        upper_half = buffer[:, middle:]
        lower = position >> level & 1 == 0
        kept = jnp.where(lower, lower_half, upper_half)
        outgoing = jnp.where(lower, upper_half, lower_half)
        incoming = partner_2(outgoing, "context", level)
        buffer = kept + incoming
    return buffer


def body(upstream, out_weight, query_rows, key_rows, value_rows, head_offsets):
    position = lax.axis_index("context")
    span_length, block_width = query_rows.shape
    head_count = block_width // HEAD_SIZE
    scale = 1.0 / math.sqrt(HEAD_SIZE)
    partial_rows = dot_rows(upstream, lax.all_gather(out_weight, "heads", axis=0, tiled=True))
    attn_grad = lax.all_to_all(
        partial_rows.astype(jnp.bfloat16), "heads", split_axis=1, concat_axis=0, tiled=True
    )
    local_shifts = lax.dynamic_slice_in_dim(
        head_offsets, lax.axis_index("heads") * head_count, head_count
    )
    mask_stack = jnp.arange(DILATION_RATE, dtype=jnp.int32)[:, None] == local_shifts[None, :]
    query_pick = pick_rows(query_rows, mask_stack)
    grad_pick = pick_rows(attn_grad, mask_stack)
    key_pick = pick_rows(key_rows, mask_stack)
    value_pick = pick_rows(value_rows, mask_stack)
    picked_pair = jnp.stack([key_pick, value_pick])
    dense_span = FIRST_SEGMENT // span_length
    dense_levels = dense_span.bit_length() - 1
    near_pair = double_up(jnp.stack([key_rows, value_rows]), dense_levels, position)
    far_pair = lax.all_gather(picked_pair, "context", axis=1, tiled=True)
    block_rows = min(512, span_length)
    num_blocks = span_length // block_rows
    current_row_index = jnp.arange(span_length, dtype=jnp.int32)
    dq_near_list, dk_near_list, dv_near_list = ([], [], [])
    dq_far_list, dk_far_list, dv_far_list = ([], [], [])
    lse_list, delta_list = ([], [])
    for head in range(head_count):
        columns = slice(head * HEAD_SIZE, (head + 1) * HEAD_SIZE)
        head_shift = local_shifts[head]
        query_head = query_rows[:, columns]
        grad_head = attn_grad[:, columns]
        near_keys = near_pair[0][:, columns]
        near_values = near_pair[1][:, columns]
        query_sel = query_pick[:, columns]
        grad_sel = grad_pick[:, columns]
        far_keys = far_pair[0][:, columns]
        far_values = far_pair[1][:, columns]
        score_near = dot_rows(query_sel, near_keys) * scale
        score_far = dot_rows(query_sel, far_keys) * scale
        row_max = jnp.maximum(jnp.max(score_near, 1), jnp.max(score_far, 1))
        row_sum = jnp.sum(jnp.exp(score_near - row_max[:, None]), 1) + jnp.sum(
            jnp.exp(score_far - row_max[:, None]), 1
        )
        lse_sel = row_max + jnp.log(row_sum)
        prob_near = jnp.exp(score_near - lse_sel[:, None])
        prob_far = jnp.exp(score_far - lse_sel[:, None])
        dprob_near = dot_rows(grad_sel, near_values)
        dprob_far = dot_rows(grad_sel, far_values)
        delta_sel = jnp.sum(prob_near * dprob_near, 1) + jnp.sum(prob_far * dprob_far, 1)
        dscore_far = (prob_far * (dprob_far - delta_sel[:, None])).astype(jnp.bfloat16)
        dq_far_list.append(
            jnp.dot(dscore_far, far_keys, preferred_element_type=jnp.float32) * scale
        )
        lse_list.append(lse_sel)
        delta_list.append(delta_sel)
        prob_far16 = prob_far.astype(jnp.bfloat16)
        dk_far_list.append(dot_cols(dscore_far, query_sel) * scale)
        dv_far_list.append(dot_cols(prob_far16, grad_sel))
        lse_rows = spread_rows(lse_sel, head_shift)
        delta_rows = spread_rows(delta_sel, head_shift)
        selected_rows = current_row_index % DILATION_RATE == head_shift

        def step(carry, inputs):
            key_acc, value_acc = carry
            query_blk, grad_blk, lse_blk, delta_blk, mask_blk = inputs
            scores = dot_rows(query_blk, near_keys) * scale
            blk_max = jnp.max(scores, 1)
            blk_sum = jnp.sum(jnp.exp(scores - blk_max[:, None]), 1)
            lse_all = jnp.where(mask_blk, lse_blk, blk_max + jnp.log(blk_sum))
            probs = jnp.exp(scores - lse_all[:, None])
            dprobs = dot_rows(grad_blk, near_values)
            delta_all = jnp.where(mask_blk, delta_blk, jnp.sum(probs * dprobs, 1))
            dscores = (probs * (dprobs - delta_all[:, None])).astype(jnp.bfloat16)
            probs16 = probs.astype(jnp.bfloat16)
            dq_blk = jnp.dot(dscores, near_keys, preferred_element_type=jnp.float32) * scale
            key_acc = key_acc + dot_cols(dscores, query_blk) * scale
            value_acc = value_acc + dot_cols(probs16, grad_blk)
            return ((key_acc, value_acc), dq_blk)

        zeros_acc = jnp.zeros((near_keys.shape[0], HEAD_SIZE), jnp.float32)
        (key_acc, value_acc), dq_blocks = lax.scan(
            step,
            (zeros_acc, zeros_acc),
            (
                query_head.reshape(num_blocks, block_rows, HEAD_SIZE),
                grad_head.reshape(num_blocks, block_rows, HEAD_SIZE),
                lse_rows.reshape(num_blocks, block_rows),
                delta_rows.reshape(num_blocks, block_rows),
                selected_rows.reshape(num_blocks, block_rows),
            ),
        )
        dq_near_list.append(dq_blocks.reshape(span_length, HEAD_SIZE))
        dk_near_list.append(key_acc)
        dv_near_list.append(value_acc)
    near_terms = jnp.stack([jnp.concatenate(dk_near_list, 1), jnp.concatenate(dv_near_list, 1)])
    near_back = halve_down(near_terms, dense_levels, position)
    far_terms = jnp.stack([jnp.concatenate(dk_far_list, 1), jnp.concatenate(dv_far_list, 1)])
    far_back = lax.psum_scatter(far_terms, "context", scatter_dimension=1, tiled=True)
    far_key_grad = far_back[0]
    far_value_grad = far_back[1]
    query_grad = (
        jnp.concatenate(dq_near_list, 1) + place_rows(jnp.concatenate(dq_far_list, 1), mask_stack)
    ).astype(jnp.bfloat16)
    key_grad = (near_back[0] + place_rows(far_key_grad, mask_stack)).astype(jnp.bfloat16)
    value_grad = (near_back[1] + place_rows(far_value_grad, mask_stack)).astype(jnp.bfloat16)
    return (query_grad, key_grad, value_grad)


def solution(mesh):
    return jax.shard_map(
        body,
        mesh=mesh,
        in_specs=(
            P(("context", "heads"), None),
            P("heads", None),
            P("context", "heads"),
            P("context", "heads"),
            P("context", "heads"),
            P(),
        ),
        out_specs=(P("context", "heads"), P("context", "heads"), P("context", "heads")),
        check_vma=False,
    )
```

profile of v0, /device:TPU:4, one launch (start us, length us, event | category | flops | bytes accessed | tf_op | source)
XLA Modules:
  0.0 1150.2 jit_solution(13889192455797140097)
XLA Ops:
  8.3 2.0 collective-permute-start
  10.4 6.2 collective-permute-done
  17.9 3.4 collective-permute-start.1
  21.2 22.5 %collective-permute-done.1 = bf16[2,512,256]{2,1,0:T(8,128)(2,1)S(1)} collective-permute-done((bf16[2,512,256]{2,1,0:T(8,128)(2,1)S(1)}, bf16[2,512,256]{2,1,0:T(8,128)(2,1)S(1)}, u32[]{:S(2)}, u32[]{:S(2)}) %collective-permute-start.1) | collective-permute-done | bytes 524320 | tf_op jit(solution)/shard_map/ppermute | solution.py:15
  44.0 6.3 collective-permute-start.2
  59.5 36.6 %collective-permute-done.2 = bf16[2,1024,256]{2,1,0:T(8,128)(2,1)S(1)} collective-permute-done((bf16[2,1024,256]{2,1,0:T(8,128)(2,1)S(1)}, bf16[2,1024,256]{2,1,0:T(8,128)(2,1)S(1)}, u32[]{:S(2)}, u32[]{:S(2)}) %collective-permute-start.2) | collective-permute-done | bytes 1048608 | tf_op jit(solution)/shard_map/ppermute | solution.py:15
  97.7 1.9 fusion.135
  100.2 2.3 convolution_convert_fusion
  103.2 4.8 all-to-all-start
  108.0 2.5 exponential_reduce_fusion
  111.8 2.0 select_reduce_fusion.3
  123.2 1.6 fusion.131
  126.4 1.6 fusion.127
  128.0 284.4 %all-gather.3.cloned.1.call-done = bf16[2,1024,256]{2,1,0:T(8,128)(2,1)} async-done(((bf16[2,16,256]{2,1,0:T(8,128)(2,1)}), bf16[2,1024,256]{2,1,0:T(8,128)(2,1)}) %all-gather.3.cloned.1.call-update) | async-done | bytes 1048592 | tf_op jit(solution)/shard_map/all_gather | solution.py:104
  417.2 1.8 fusion.9
  421.9 1.6 multiply_reduce_fusion.2
  432.8 2.9 fusion.16
  435.7 3.5 fusion.1
  443.8 2.4 fusion.3
  449.8 2.9 fusion.14
  452.8 3.6 fusion.5
  459.9 2.8 fusion.13
  462.8 3.5 fusion.7
  476.8 2.8 fusion.2
  488.3 1.9 broadcast_select_fusion
  491.6 1.6 pad_maximum_fusion.1
  493.2 4.1 copy.51
  501.9 51.9 %collective-permute-done.3 = f32[2,1024,256]{1,2,0:T(8,128)} collective-permute-done((f32[2,1024,256]{1,2,0:T(8,128)}, f32[2,1024,256]{1,2,0:T(8,128)}, u32[]{:S(2)}, u32[]{:S(2)}) %collective-permute-start.3) | collective-permute-done | bytes 2097184 | tf_op jit(solution)/shard_map/ppermute | solution.py:15
  553.8 2.9 select_add_fusion
  562.3 22.9 %collective-permute-done.4 = f32[2,512,256]{1,2,0:T(8,128)S(1)} collective-permute-done((f32[2,512,256]{1,2,0:T(8,128)S(1)}, f32[2,512,256]{1,2,0:T(8,128)S(1)}, u32[]{:S(2)}, u32[]{:S(2)}) %collective-permute-start.4) | collective-permute-done | bytes 1048608 | tf_op jit(solution)/shard_map/ppermute | solution.py:15
  586.5 2.3 collective-permute-start.5
  588.9 548.2 %all-reduce.3.cloned.1.call-done = f32[2,1024,256]{2,0,1:T(2,128)} async-done(((f32[2,1024,256]{2,0,1:T(2,128)}), f32[2,1024,256]{2,0,1:T(2,128)}) %all-reduce.3.cloned.1.call-update) | async-done | bytes 2097168
  (330 shorter events, 92.7 us)
Async XLA Ops:
  7.2 93.0 %copy-start = (bf16[64,1024]{1,0:T(8,128)(2,1)S(1)}, bf16[64,1024]{1,0:T(8,128)(2,1)}, u32[]{:S(2)}) copy-start(bf16[64,1024]{1,0:T(8,128)(2,1)} %param.6) | copy-start | bytes 393220
  7.2 93.0 %all-gather.5.cloned.1.call-start = ((), (), s32[]{:S(2)}) async-start(), calls=%async_computation.2 | async-start | bytes 2621440 | tf_op jit(solution)/shard_map/all_gather | solution.py:88
  7.2 43.0 %copy-start.35 = (bf16[256,256]{1,0:T(8,128)(2,1)S(1)}, bf16[256,256]{1,0:T(8,128)(2,1)}, u32[]{:S(2)}) copy-start(bf16[256,256]{1,0:T(8,128)(2,1)} %param.9) | copy-start | bytes 393220
  8.3 42.8 %copy-start.36 = (bf16[256,256]{1,0:T(8,128)(2,1)S(1)}, bf16[256,256]{1,0:T(8,128)(2,1)}, u32[]{:S(2)}) copy-start(bf16[256,256]{1,0:T(8,128)(2,1)} %param.10) | copy-start | bytes 393220
  8.3 8.3 collective-permute-start
  10.3 41.7 %copy-start.24 = (bf16[256,256]{1,0:T(8,128)(2,1)S(1)}, bf16[256,256]{1,0:T(8,128)(2,1)}, u32[]{:S(2)}) copy-start(bf16[256,256]{1,0:T(8,128)(2,1)} %param.8) | copy-start | bytes 393220
  10.4 42.5 %copy-start.92 = (u32[256]{0:T(256)S(1)}, u32[256]{0:T(256)}, u32[]{:S(2)}) copy-start(u32[256]{0:T(256)} %constant.137) | copy-start | bytes 3076
  10.4 43.8 %copy-start.91 = (s32[16]{0:T(128)S(1)}, s32[16]{0:T(128)}, u32[]{:S(2)}) copy-start(s32[16]{0:T(128)} %param.11) | copy-start | bytes 196
  17.9 25.8 %collective-permute-start.1 = (bf16[2,512,256]{2,1,0:T(8,128)(2,1)S(1)}, bf16[2,512,256]{2,1,0:T(8,128)(2,1)S(1)}, u32[]{:S(2)}, u32[]{:S(2)}) collective-permute-start(bf16[2,512,256]{2,1,0:T(8,128)(2,1)S(1)} %maximum_select_fusion.2), channel_id=1, source_target_pairs={{0,8},{4,12},{8,0},{12,4},{16,24},{20,28},{24,16},{28,20},{32,40},... | collective-permute-start | bytes 1572872 | tf_op jit(solution)/shard_map/ppermute | solution.py:15
  44.0 52.1 %collective-permute-start.2 = (bf16[2,1024,256]{2,1,0:T(8,128)(2,1)S(1)}, bf16[2,1024,256]{2,1,0:T(8,128)(2,1)S(1)}, u32[]{:S(2)}, u32[]{:S(2)}) collective-permute-start(bf16[2,1024,256]{2,1,0:T(8,128)(2,1)S(1)} %maximum_select_fusion.1), channel_id=1, source_target_pairs={{0,16},{4,20},{8,24},{12,28},{16,0},{20,4},{24,8},{28,12},{32,48},... | collective-permute-start | bytes 3145736 | tf_op jit(solution)/shard_map/ppermute | solution.py:15
  59.5 52.3 %copy-start.43 = (pred[16,4]{1,0:T(8,128)(4,1)}, pred[16,4]{1,0:T(8,128)(4,1)S(1)}, u32[]{:S(2)}) copy-start(pred[16,4]{1,0:T(8,128)(4,1)S(1)} %iota_compare_fusion) | copy-start | bytes 196
  99.6 8.4 copy-start.64
  100.1 14.8 %copy-start.63 = (f32[256]{0:T(256)}, f32[256]{0:T(256)S(1)}, u32[]{:S(2)}) copy-start(f32[256]{0:T(256)S(1)} %get-tuple-element.199) | copy-start | bytes 3076
  103.2 7.8 all-to-all-start
  108.0 304.4 %all-gather.3.cloned.1.call-start = ((), (), s32[]{:S(2)}) async-start(), calls=%async_computation.1 | async-start | bytes 1064960 | tf_op jit(solution)/shard_map/all_gather | solution.py:104
  114.7 1022.5 %all-reduce.3.cloned.1.call-start = ((), (), s32[]{:S(2)}) async-start(), calls=%async_computation.3 | async-start | bytes 4194304
  412.4 8.3 copy-start.34
  413.8 11.1 copy-start.12
  413.8 9.8 copy-start.89
  413.8 9.9 copy-start.33
  414.2 14.1 %copy-start.31 = (f32[16,1024]{1,0:T(8,128)}, f32[16,1024]{1,0:T(8,128)S(1)}, u32[]{:S(2)}) copy-start(f32[16,1024]{1,0:T(8,128)S(1)} %get-tuple-element.163) | copy-start | bytes 196612
  414.8 11.7 %copy-start.29 = (f32[16,1024]{1,0:T(8,128)}, f32[16,1024]{1,0:T(8,128)S(1)}, u32[]{:S(2)}) copy-start(f32[16,1024]{1,0:T(8,128)S(1)} %get-tuple-element.182) | copy-start | bytes 196612
  414.8 11.5 %copy-start.88 = (f32[16]{0:T(128)S(1)}, f32[16]{0:T(128)}, u32[]{:S(2)}) copy-start(f32[16]{0:T(128)} %get-tuple-element.160) | copy-start | bytes 196
  414.9 11.7 %copy-start.32 = (f32[16,2048]{1,0:T(8,128)S(1)}, f32[16,2048]{1,0:T(8,128)}, u32[]{:S(2)}) copy-start(f32[16,2048]{1,0:T(8,128)} %get-tuple-element.161) | copy-start | bytes 393220
  417.2 10.6 copy-start.45
  420.5 8.8 copy-start.87
  420.9 8.3 copy-start.49
  470.9 8.6 copy-start.38
  490.3 63.6 %collective-permute-start.3 = (f32[2,1024,256]{1,2,0:T(8,128)}, f32[2,1024,256]{1,2,0:T(8,128)}, u32[]{:S(2)}, u32[]{:S(2)}) collective-permute-start(f32[2,1024,256]{1,2,0:T(8,128)} %broadcast_select_fusion), channel_id=1, source_target_pairs={{0,16},{4,20},{8,24},{12,28},{16,0},{20,4},{24,8},{28,12},{32,48},... | collective-permute-start | bytes 6291464 | tf_op jit(solution)/shard_map/ppermute | solution.py:15
  557.0 28.3 %collective-permute-start.4 = (f32[2,512,256]{1,2,0:T(8,128)S(1)}, f32[2,512,256]{1,2,0:T(8,128)S(1)}, u32[]{:S(2)}, u32[]{:S(2)}) collective-permute-start(f32[2,512,256]{1,2,0:T(8,128)S(1)} %slice_select_fusion), channel_id=1, source_target_pairs={{0,8},{4,12},{8,0},{12,4},{16,24},{20,28},{24,16},{28,20},{32,40},... | collective-permute-start | bytes 3145736 | tf_op jit(solution)/shard_map/ppermute | solution.py:15
  562.3 575.9 %copy-start.44 = (pred[16,4]{1,0:T(8,128)(4,1)S(1)}, pred[16,4]{1,0:T(8,128)(4,1)}, u32[]{:S(2)}) copy-start(pred[16,4]{1,0:T(8,128)(4,1)} %copy-done.43) | copy-start | bytes 196
  586.5 555.5 %collective-permute-start.5 = (f32[2,256,256]{1,2,0:T(8,128)}, f32[2,256,256]{1,2,0:T(8,128)S(1)}, u32[]{:S(2)}, u32[]{:S(2)}) collective-permute-start(f32[2,256,256]{1,2,0:T(8,128)} %slice_select_fusion.1), channel_id=1, source_target_pairs={{0,4},{4,0},{8,12},{12,8},{16,20},{20,16},{24,28},{28,24},{32,36},... | collective-permute-start | bytes 1572872 | tf_op jit(solution)/shard_map/ppermute | solution.py:15
  (71 other events, 207.4 us)
Sparse Core Ops, SparseCore 0:
  10.5 28.7 all-gather.4
  114.8 297.5 all-gather.2
  497.4 639.6 all-reduce.2
where the time goes:
time: 1150 us
  waiting for transfers between devices  973 us (85%)
  matrix products  60 us (5%)
  other arithmetic  48.8 us (4%)
  local copies, waits for them, and re-layouts  33.5 us (3%)
  starting transfers between devices  19.1 us (2%)
  between operations  15.5 us (1%)
    unnamed x4, waiting for transfers between devices  548 us
    all_gather x1, waiting for transfers between devices, body(): far_pair = lax.all_gather(picked_pair, 'context', axis=1, tiled=True)  284 us
    ppermute x6, waiting for transfers between devices, partner_2(): return lax.ppermute(value, axis, pairs)  140 us
    dot_general x25, matrix products, dot_rows(): lax.dot_general(left, right, (((1,), (1,)), ((), ())), preferred_element_...  36.3 us
  transfers between devices with their start and end apart: 10, of which 8 were waited for; matrix products, arithmetic and copies ran while one was open for 5% of the time, Pallas kernels for 0%

commit v1 on v0

--- a/solution.py
+++ b/solution.py
@@ -101,7 +101,9 @@
     dense_span = FIRST_SEGMENT // span_length
     dense_levels = dense_span.bit_length() - 1
     near_pair = double_up(jnp.stack([key_rows, value_rows]), dense_levels, position)
-    far_pair = lax.all_gather(picked_pair, "context", axis=1, tiled=True)
+    far_pair = jnp.concatenate(
+        lax.all_to_all(jnp.stack([picked_pair] * lax.axis_size("context")), "context", 0, 0), axis=1
+    )
     block_rows = min(512, span_length)
     num_blocks = span_length // block_rows
     current_row_index = jnp.arange(span_length, dtype=jnp.int32)

time: 1150 us -> 917 us (0.80)
  waiting for transfers between devices: 973 us -> 696 us
  starting transfers between devices: 19.1 us -> 61.5 us
    all_gather x1 -> x0, waiting for transfers between devices: 284 us -> none  [body(): far_pair = lax.all_gather(picked_pair, 'context', axis=1, tiled=True)]
    ppermute x6, starting transfers between devices: 14.1 us -> 47.6 us  [partner_2(): return lax.ppermute(value, axis, pairs)]
    unnamed x4 -> x3, waiting for transfers between devices: 548 us -> 519 us
    ppermute x6, waiting for transfers between devices: 140 us -> 161 us  [partner_2(): return lax.ppermute(value, axis, pairs)]
    all_to_all x0 -> x1, waiting for transfers between devices: none -> 15.6 us  [body(): lax.all_to_all(jnp.stack([picked_pair] * lax.axis_size('context')), 'cont...]
  transfers between devices with their start and end apart: 10 -> 10, of which waited for: 8 -> 8; matrix products, arithmetic and copies ran while one was open for 5% -> 6% of each run, Pallas kernels for 0% -> 0%
where the time goes in v1:
time: 917 us; the launch traced here: 915 us
  waiting for transfers between devices  696 us (76%)
  starting transfers between devices  61.5 us (7%)
  matrix products  60 us (7%)
  other arithmetic  48.3 us (5%)
  local copies, waits for them, and re-layouts  33.7 us (4%)
  between operations  16 us (2%)
    unnamed x3, waiting for transfers between devices  519 us
    ppermute x6, waiting for transfers between devices, partner_2(): return lax.ppermute(value, axis, pairs)  161 us
    ppermute x6, starting transfers between devices, partner_2(): return lax.ppermute(value, axis, pairs)  47.6 us
    dot_general x25, matrix products, dot_rows(): lax.dot_general(left, right, (((1,), (1,)), ((), ())), preferred_element_...  36.3 us
  transfers between devices with their start and end apart: 10, of which 8 were waited for; matrix products, arithmetic and copies ran while one was open for 6% of the time, Pallas kernels for 0%

profile of v1, /device:TPU:4, one launch (start us, length us, event | category | flops | bytes accessed | tf_op | source)
XLA Modules:
  0.0 915.1 jit_solution(14876698733321965472)
XLA Ops:
  8.3 2.0 collective-permute-start
  10.4 6.2 collective-permute-done
  17.9 3.4 collective-permute-start.1
  21.2 22.5 %collective-permute-done.1 = bf16[2,512,256]{2,1,0:T(8,128)(2,1)S(1)} collective-permute-done((bf16[2,512,256]{2,1,0:T(8,128)(2,1)S(1)}, bf16[2,512,256]{2,1,0:T(8,128)(2,1)S(1)}, u32[]{:S(2)}, u32[]{:S(2)}) %collective-permute-start.1) | collective-permute-done | bytes 524320 | tf_op jit(solution)/shard_map/ppermute | solution.py:15
  44.0 6.3 collective-permute-start.2
  59.5 36.5 %collective-permute-done.2 = bf16[2,1024,256]{2,1,0:T(8,128)(2,1)S(1)} collective-permute-done((bf16[2,1024,256]{2,1,0:T(8,128)(2,1)S(1)}, bf16[2,1024,256]{2,1,0:T(8,128)(2,1)S(1)}, u32[]{:S(2)}, u32[]{:S(2)}) %collective-permute-start.2) | collective-permute-done | bytes 1048608 | tf_op jit(solution)/shard_map/ppermute | solution.py:15
  97.7 1.9 fusion.136
  100.2 2.3 convolution_convert_fusion
  103.2 4.8 all-to-all-start.1
  108.0 2.5 exponential_reduce_fusion
  111.8 2.0 select_reduce_fusion.3
  115.2 8.9 all-to-all-start
  135.7 1.6 fusion.128
  137.3 15.6 %all-to-all-done = bf16[64,2,16,256]{3,2,1,0:T(8,128)(2,1)} async-done(((bf16[64,2,16,256]{3,2,1,0:T(8,128)(2,1)}), bf16[64,2,16,256]{3,2,1,0:T(8,128)(2,1)}, u32[]{:S(2)}, u32[]{:S(2)}) %all-to-all-start) | async-done | bytes 1048608 | tf_op jit(solution)/shard_map/all_to_all | solution.py:105
  157.7 1.9 fusion.9
  173.4 3.0 fusion.16
  176.4 3.5 fusion.1
  184.6 2.4 fusion.3
  190.5 2.9 fusion.14
  193.5 3.5 fusion.5
  200.5 2.9 fusion.13
  203.4 3.5 fusion.7
  217.4 2.8 fusion.2
  229.1 1.9 broadcast_select_fusion
  231.0 2.4 collective-permute-start.3
  234.7 1.6 pad_maximum_fusion.1
  236.3 4.1 copy.51
  245.1 52.0 %collective-permute-done.3 = f32[2,1024,256]{1,2,0:T(8,128)} collective-permute-done((f32[2,1024,256]{1,2,0:T(8,128)}, f32[2,1024,256]{1,2,0:T(8,128)}, u32[]{:S(2)}, u32[]{:S(2)}) %collective-permute-start.3) | collective-permute-done | bytes 2097184 | tf_op jit(solution)/shard_map/ppermute | solution.py:15
  297.1 2.9 select_add_fusion
  300.2 33.6 %collective-permute-start.4 = (f32[2,512,256]{1,2,0:T(8,128)S(1)}, f32[2,512,256]{1,2,0:T(8,128)S(1)}, u32[]{:S(2)}, u32[]{:S(2)}) collective-permute-start(f32[2,512,256]{1,2,0:T(8,128)S(1)} %slice_select_fusion), channel_id=1, source_target_pairs={{0,8},{4,12},{8,0},{12,4},{16,24},{20,28},{24,16},{28,20},{32,40},... | collective-permute-start | bytes 3145736 | tf_op jit(solution)/shard_map/ppermute | solution.py:15
  338.2 43.3 %collective-permute-done.4 = f32[2,512,256]{1,2,0:T(8,128)S(1)} collective-permute-done((f32[2,512,256]{1,2,0:T(8,128)S(1)}, f32[2,512,256]{1,2,0:T(8,128)S(1)}, u32[]{:S(2)}, u32[]{:S(2)}) %collective-permute-start.4) | collective-permute-done | bytes 1048608 | tf_op jit(solution)/shard_map/ppermute | solution.py:15
  382.9 519.0 %all-reduce.3.cloned.1.call-done = f32[2,1024,256]{2,0,1:T(2,128)} async-done(((f32[2,1024,256]{2,0,1:T(2,128)}), f32[2,1024,256]{2,0,1:T(2,128)}) %all-reduce.3.cloned.1.call-update) | async-done | bytes 2097168
  (330 shorter events, 95.4 us)
Async XLA Ops:
  7.2 93.0 %copy-start = (bf16[64,1024]{1,0:T(8,128)(2,1)S(1)}, bf16[64,1024]{1,0:T(8,128)(2,1)}, u32[]{:S(2)}) copy-start(bf16[64,1024]{1,0:T(8,128)(2,1)} %param.6) | copy-start | bytes 393220
  7.2 93.0 %all-gather.2.cloned.1.call-start = ((), (), s32[]{:S(2)}) async-start(), calls=%async_computation.2 | async-start | bytes 2621440 | tf_op jit(solution)/shard_map/all_gather | solution.py:88
  7.2 43.0 %copy-start.35 = (bf16[256,256]{1,0:T(8,128)(2,1)S(1)}, bf16[256,256]{1,0:T(8,128)(2,1)}, u32[]{:S(2)}) copy-start(bf16[256,256]{1,0:T(8,128)(2,1)} %param.9) | copy-start | bytes 393220
  8.3 42.8 %copy-start.36 = (bf16[256,256]{1,0:T(8,128)(2,1)S(1)}, bf16[256,256]{1,0:T(8,128)(2,1)}, u32[]{:S(2)}) copy-start(bf16[256,256]{1,0:T(8,128)(2,1)} %param.10) | copy-start | bytes 393220
  8.3 8.3 collective-permute-start
  10.3 41.7 %copy-start.24 = (bf16[256,256]{1,0:T(8,128)(2,1)S(1)}, bf16[256,256]{1,0:T(8,128)(2,1)}, u32[]{:S(2)}) copy-start(bf16[256,256]{1,0:T(8,128)(2,1)} %param.8) | copy-start | bytes 393220
  10.4 42.5 %copy-start.92 = (u32[256]{0:T(256)S(1)}, u32[256]{0:T(256)}, u32[]{:S(2)}) copy-start(u32[256]{0:T(256)} %constant.137) | copy-start | bytes 3076
  10.4 43.7 %copy-start.91 = (s32[16]{0:T(128)S(1)}, s32[16]{0:T(128)}, u32[]{:S(2)}) copy-start(s32[16]{0:T(128)} %param.11) | copy-start | bytes 196
  17.9 25.8 %collective-permute-start.1 = (bf16[2,512,256]{2,1,0:T(8,128)(2,1)S(1)}, bf16[2,512,256]{2,1,0:T(8,128)(2,1)S(1)}, u32[]{:S(2)}, u32[]{:S(2)}) collective-permute-start(bf16[2,512,256]{2,1,0:T(8,128)(2,1)S(1)} %maximum_select_fusion.2), channel_id=1, source_target_pairs={{0,8},{4,12},{8,0},{12,4},{16,24},{20,28},{24,16},{28,20},{32,40},... | collective-permute-start | bytes 1572872 | tf_op jit(solution)/shard_map/ppermute | solution.py:15
  44.0 52.1 %collective-permute-start.2 = (bf16[2,1024,256]{2,1,0:T(8,128)(2,1)S(1)}, bf16[2,1024,256]{2,1,0:T(8,128)(2,1)S(1)}, u32[]{:S(2)}, u32[]{:S(2)}) collective-permute-start(bf16[2,1024,256]{2,1,0:T(8,128)(2,1)S(1)} %maximum_select_fusion.1), channel_id=1, source_target_pairs={{0,16},{4,20},{8,24},{12,28},{16,0},{20,4},{24,8},{28,12},{32,48},... | collective-permute-start | bytes 3145736 | tf_op jit(solution)/shard_map/ppermute | solution.py:15
  59.5 52.3 %copy-start.43 = (pred[16,4]{1,0:T(8,128)(4,1)}, pred[16,4]{1,0:T(8,128)(4,1)S(1)}, u32[]{:S(2)}) copy-start(pred[16,4]{1,0:T(8,128)(4,1)S(1)} %iota_compare_fusion) | copy-start | bytes 196
  100.1 24.1 %copy-start.63 = (f32[256]{0:T(256)}, f32[256]{0:T(256)S(1)}, u32[]{:S(2)}) copy-start(f32[256]{0:T(256)S(1)} %get-tuple-element.199) | copy-start | bytes 3076
  103.2 7.8 all-to-all-start.1
  115.2 37.8 %all-to-all-start = ((bf16[64,2,16,256]{3,2,1,0:T(8,128)(2,1)}), bf16[64,2,16,256]{3,2,1,0:T(8,128)(2,1)}, u32[]{:S(2)}, u32[]{:S(2)}) async-start(bf16[64,2,16,256]{3,2,1,0:T(8,128)(2,1)} %stack.26), calls=%async_computation | async-start | bytes 2097152 | tf_op jit(solution)/shard_map/all_to_all | solution.py:105
  124.0 777.8 %all-reduce.3.cloned.1.call-start = ((), (), s32[]{:S(2)}) async-start(), calls=%async_computation.3 | async-start | bytes 4194304
  154.4 11.1 %copy-start.12 = (bf16[1,64,16,256]{3,2,0,1:T(8,128)(2,1)}, bf16[1,64,16,256]{3,2,0,1:T(8,128)(2,1)S(1)}, u32[]{:S(2)}) copy-start(bf16[1,64,16,256]{3,2,0,1:T(8,128)(2,1)S(1)} %get-tuple-element.119) | copy-start | bytes 1572868
  154.4 9.7 %copy-start.89 = (f32[16]{0:T(128)S(1)}, f32[16]{0:T(128)}, u32[]{:S(2)}) copy-start(f32[16]{0:T(128)} %get-tuple-element.164) | copy-start | bytes 196
  154.4 9.9 %copy-start.33 = (f32[16,2048]{1,0:T(8,128)S(1)}, f32[16,2048]{1,0:T(8,128)}, u32[]{:S(2)}) copy-start(f32[16,2048]{1,0:T(8,128)} %get-tuple-element.176) | copy-start | bytes 393220
  154.8 14.1 %copy-start.31 = (f32[16,1024]{1,0:T(8,128)}, f32[16,1024]{1,0:T(8,128)S(1)}, u32[]{:S(2)}) copy-start(f32[16,1024]{1,0:T(8,128)S(1)} %get-tuple-element.163) | copy-start | bytes 196612
  155.4 11.7 %copy-start.29 = (f32[16,1024]{1,0:T(8,128)}, f32[16,1024]{1,0:T(8,128)S(1)}, u32[]{:S(2)}) copy-start(f32[16,1024]{1,0:T(8,128)S(1)} %get-tuple-element.182) | copy-start | bytes 196612
  155.5 11.5 %copy-start.88 = (f32[16]{0:T(128)S(1)}, f32[16]{0:T(128)}, u32[]{:S(2)}) copy-start(f32[16]{0:T(128)} %get-tuple-element.160) | copy-start | bytes 196
  155.5 11.7 %copy-start.32 = (f32[16,2048]{1,0:T(8,128)S(1)}, f32[16,2048]{1,0:T(8,128)}, u32[]{:S(2)}) copy-start(f32[16,2048]{1,0:T(8,128)} %get-tuple-element.161) | copy-start | bytes 393220
  157.7 10.7 %copy-start.45 = (f32[16]{0:T(128)}, f32[16]{0:T(128)S(1)}, u32[]{:S(2)}) copy-start(f32[16]{0:T(128)S(1)} %log_add_fusion.3) | copy-start | bytes 196
  161.1 8.8 copy-start.87
  231.0 66.1 %collective-permute-start.3 = (f32[2,1024,256]{1,2,0:T(8,128)}, f32[2,1024,256]{1,2,0:T(8,128)}, u32[]{:S(2)}, u32[]{:S(2)}) collective-permute-start(f32[2,1024,256]{1,2,0:T(8,128)} %broadcast_select_fusion), channel_id=1, source_target_pairs={{0,16},{4,20},{8,24},{12,28},{16,0},{20,4},{24,8},{28,12},{32,48},... | collective-permute-start | bytes 6291464 | tf_op jit(solution)/shard_map/ppermute | solution.py:15
  300.0 33.8 %copy-start.14 = (bf16[256,2048]{0,1:T(8,128)(2,1)S(1)}, bf16[256,2048]{0,1:T(8,128)(2,1)}, u32[]{:S(2)}) copy-start(bf16[256,2048]{0,1:T(8,128)(2,1)} %copy-done.13) | copy-start | bytes 3145732
  300.0 35.0 %copy-start.16 = (bf16[256,2048]{0,1:T(8,128)(2,1)S(1)}, bf16[256,2048]{0,1:T(8,128)(2,1)}, u32[]{:S(2)}) copy-start(bf16[256,2048]{0,1:T(8,128)(2,1)} %copy-done.15) | copy-start | bytes 3145732
  300.2 35.8 %copy-start.18 = (bf16[256,2048]{0,1:T(8,128)(2,1)S(1)}, bf16[256,2048]{0,1:T(8,128)(2,1)}, u32[]{:S(2)}) copy-start(bf16[256,2048]{0,1:T(8,128)(2,1)} %copy-done.17) | copy-start | bytes 3145732
  300.2 37.0 %copy-start.20 = (bf16[256,2048]{0,1:T(8,128)(2,1)S(1)}, bf16[256,2048]{0,1:T(8,128)(2,1)}, u32[]{:S(2)}) copy-start(bf16[256,2048]{0,1:T(8,128)(2,1)} %copy-done.19) | copy-start | bytes 3145732
  300.2 81.2 %collective-permute-start.4 = (f32[2,512,256]{1,2,0:T(8,128)S(1)}, f32[2,512,256]{1,2,0:T(8,128)S(1)}, u32[]{:S(2)}, u32[]{:S(2)}) collective-permute-start(f32[2,512,256]{1,2,0:T(8,128)S(1)} %slice_select_fusion), channel_id=1, source_target_pairs={{0,8},{4,12},{8,0},{12,4},{16,24},{20,28},{24,16},{28,20},{32,40},... | collective-permute-start | bytes 3145736 | tf_op jit(solution)/shard_map/ppermute | solution.py:15
  338.2 564.7 %copy-start.44 = (pred[16,4]{1,0:T(8,128)(4,1)S(1)}, pred[16,4]{1,0:T(8,128)(4,1)}, u32[]{:S(2)}) copy-start(pred[16,4]{1,0:T(8,128)(4,1)} %copy-done.43) | copy-start | bytes 196
  382.7 523.9 %collective-permute-start.5 = (f32[2,256,256]{1,2,0:T(8,128)}, f32[2,256,256]{1,2,0:T(8,128)S(1)}, u32[]{:S(2)}, u32[]{:S(2)}) collective-permute-start(f32[2,256,256]{1,2,0:T(8,128)} %slice_select_fusion.1), channel_id=1, source_target_pairs={{0,4},{4,0},{8,12},{12,8},{16,20},{20,16},{24,28},{28,24},{32,36},... | collective-permute-start | bytes 1572872 | tf_op jit(solution)/shard_map/ppermute | solution.py:15
  (71 other events, 242.2 us)
Sparse Core Ops, SparseCore 0:
  10.5 28.7 all-gather.1
  240.6 661.2 all-reduce.2
